TPU v7x, 512 devices: a whole 4x4x16 slice. The times are simulated.
512 devices in a mesh: rep: 64 (over x_lo, z, core), tp: 8 (over y, x_hi).
Axes of the slice: x: 4 (x_hi: 2, x_lo: 2; x = x_hi * 2 + x_lo), y: 4, z: 16, core: 2. Of those that a mesh axis runs over, the one named last changes fastest.
Arguments:
- prompt_q: bfloat16 [32768, 2048], P('rep', 'tp'), may hold values from -24 to 24
- prompt_k: bfloat16 [32768, 2048], P('rep', 'tp'), may hold values from -24 to 24
- prompt_v: bfloat16 [32768, 2048], P('rep', 'tp'), may hold values from -6 to 6
- prompt_len: int32 [64], P('rep'), may hold values from 256 to 512, as said below
- cache_keys: bfloat16 [128, 1024, 2048], P('rep', None, 'tp'), may hold values from -24 to 24
- cache_values: bfloat16 [128, 1024, 2048], P('rep', None, 'tp'), may hold values from -6 to 6
- new_q: bfloat16 [128, 2048], P('rep', 'tp'), may hold values from -24 to 24
- new_k: bfloat16 [128, 2048], P('rep', 'tp'), may hold values from -6 to 6
- new_v: bfloat16 [128, 2048], P('rep', 'tp'), may hold values from -6 to 6
- cache_len: int32 [128], replicated, may hold values from 260 to 1024, as said below
- moving: int32 [64], replicated, may hold values from 0 to 1
- out_weight: bfloat16 [2048, 2048], P(None, 'tp'), may hold values from -0.125 to 0.125
- out_bias: float32 [2048], P('tp'), may hold values from -1.75 to 1.75
- residual: bfloat16 [32896, 2048], P('rep', 'tp'), may hold values from -150 to 150
- ln_gain: float32 [2048], P('tp'), may hold values from 0.1 to 1.9
- ln_shift: float32 [2048], P('tp'), may hold values from -1.75 to 1.75
Outputs:
- hidden_out: bfloat16 [32896, 2048], P('rep', 'tp')
- normed: bfloat16 [32896, 2048], P('rep', 'tp')
- moved_window: bfloat16 [64, 2, 260, 2048], P('rep', None, None, 'tp')
Inputs may be any that keep to these rules, and one draw needn't show every extreme that they name: `prompt_len`: some replica's prompt has all 512 tokens live. `cache_len`: some request's cache is full.
All inputs are finite; a program needn't handle non-finite values.
Results may differ from a plain program's by a relative error of at most 0.0022.
Values may be sent and summed in bfloat16 or wider, within the bound.
No kernel may reach another device: no remote copies, remote signals or barrier semaphores. Data moves between devices by JAX's collectives and lax.ppermute only.
A program may use at most 64 MiB of HBM per device.

v0:
```python
import math
import jax
import jax.numpy as jnp
from jax import lax
from jax.sharding import PartitionSpec as P

D = 2048
HEADS = 16
HD = 128
SINK = 4
WIN = 256
masked_score = -1e30
norm_epsilon = 1e-05


def from_behind(block, axis, distance):
    devices = range(lax.axis_size(axis))
    route = [((i - distance) % len(devices), i) for i in devices]
    return lax.ppermute(block, axis, route)


def head_slopes(local_heads):
    first_head = lax.axis_index("tp") * local_heads
    head_ids = (first_head + jnp.arange(local_heads, dtype=jnp.int32)).astype(jnp.float32)
    return jnp.exp2(-8.0 * (head_ids + 1.0) / HEADS)


def softmax_rows(scores):
    row_max = jnp.max(scores, axis=-1, keepdims=True)
    expo_terms = jnp.exp(scores - row_max)
    return (expo_terms / jnp.sum(expo_terms, axis=-1, keepdims=True)).astype(jnp.bfloat16)


def prompt_attend(query_rows, key_rows, value_rows, length, slopes):
    row_count = query_rows.shape[0]
    local_heads = slopes.shape[0]
    query_heads = query_rows.reshape(row_count, local_heads, HD)
    key_heads = key_rows.reshape(row_count, local_heads, HD)
    value_heads = value_rows.reshape(row_count, local_heads, HD)
    scores = jnp.einsum(
        "qhd,khd->hqk", query_heads, key_heads, preferred_element_type=jnp.float32
    ) * (1.0 / math.sqrt(HD))
    position = jnp.arange(row_count, dtype=jnp.int32)
    distance = (position[:, None] - position[None, :]).astype(jnp.float32)
    scores = scores - slopes[:, None, None] * distance[None]
    allowed = (position[None, :] <= position[:, None]) & (position[None, :] < length)
    scores = jnp.where(allowed[None], scores, masked_score)
    weights = softmax_rows(scores)
    mixed_heads = jnp.einsum(
        "hqk,khd->qhd", weights, value_heads, preferred_element_type=jnp.float32
    )
    return mixed_heads.astype(jnp.bfloat16).reshape(row_count, local_heads * HD)


def window_rows(cache_rows, newest, length):
    middle = lax.dynamic_slice_in_dim(cache_rows, length + 1 - WIN, WIN - 1, 0)
    return jnp.concatenate([cache_rows[:SINK], middle, newest[None]], axis=0)


def window_positions(length):
    sink_part = jnp.arange(SINK, dtype=jnp.int32)
    tail_part = length + 1 - WIN + jnp.arange(WIN, dtype=jnp.int32)
    return jnp.concatenate([sink_part, tail_part])


def decode_attend(query_row, key_window, value_window, length, slopes):
    local_heads = slopes.shape[0]
    query_heads = query_row.reshape(local_heads, HD)
    key_heads = key_window.reshape(-1, local_heads, HD)
    value_heads = value_window.reshape(-1, local_heads, HD)
    scores = jnp.einsum(
        "hd,whd->hw", query_heads, key_heads, preferred_element_type=jnp.float32
    ) * (1.0 / math.sqrt(HD))
    distance = (length - window_positions(length)).astype(jnp.float32)
    scores = scores - slopes[:, None] * distance[None, :]
    weights = softmax_rows(scores)
    mixed_heads = jnp.einsum("hw,whd->hd", weights, value_heads, preferred_element_type=jnp.float32)
    return mixed_heads.astype(jnp.bfloat16).reshape(local_heads * HD)


def select_slot(stacked, slot_index):
    return lax.dynamic_index_in_dim(stacked, slot_index, 0, keepdims=False)


def on_device(
    prompt_q,
    prompt_k,
    prompt_v,
    prompt_len,
    cache_keys,
    cache_values,
    new_q,
    new_k,
    new_v,
    cache_len,
    moving,
    out_weight,
    out_bias,
    residual,
    ln_gain,
    ln_shift,
):
    replica_count = lax.axis_size("rep")
    replica_index = lax.axis_index("rep")
    partner = (replica_index + replica_count // 2) % replica_count
    local_heads = prompt_q.shape[1] // HD
    slopes = head_slopes(local_heads)
    prompt_mix = prompt_attend(prompt_q, prompt_k, prompt_v, prompt_len[0], slopes)
    slot_count = cache_keys.shape[0]
    leaving = moving[replica_index]
    staying = 1 - leaving
    stay_len = cache_len[replica_index * slot_count + staying]
    come_len = cache_len[partner * slot_count + moving[partner]]
    stay_keys = window_rows(select_slot(cache_keys, staying), select_slot(new_k, staying), stay_len)
    stay_values = window_rows(
        select_slot(cache_values, staying), select_slot(new_v, staying), stay_len
    )
    stay_out = decode_attend(select_slot(new_q, staying), stay_keys, stay_values, stay_len, slopes)
    come_cache_keys, come_cache_values, come_query, come_key, come_value = from_behind(
        (
            select_slot(cache_keys, leaving),
            select_slot(cache_values, leaving),
            select_slot(new_q, leaving),
            select_slot(new_k, leaving),
            select_slot(new_v, leaving),
        ),
        "rep",
        replica_count // 2,
    )
    come_keys = window_rows(come_cache_keys, come_key, come_len)
    come_values = window_rows(come_cache_values, come_value, come_len)
    come_out = decode_attend(come_query, come_keys, come_values, come_len, slopes)
    mixed_rows = jnp.concatenate([prompt_mix, stay_out[None], come_out[None]], axis=0)
    projected = jnp.dot(
        lax.all_gather(mixed_rows, "tp", axis=1, tiled=True),
        out_weight,
        preferred_element_type=jnp.float32,
    )
    stream = projected + out_bias[None, :] + residual.astype(jnp.float32)
    hidden_out = stream.astype(jnp.bfloat16)
    row_total = jnp.sum(stream, axis=1)
    row_mean = lax.psum(row_total, "tp") / D
    centered = stream - row_mean[:, None]
    row_var = lax.psum(jnp.sum(centered * centered, axis=1), "tp") / D
    normed = (
        centered * lax.rsqrt(row_var + norm_epsilon)[:, None] * ln_gain[None, :] + ln_shift[None, :]
    ).astype(jnp.bfloat16)
    moved_window = jnp.stack([come_keys, come_values], axis=0)[None]
    return (hidden_out, normed, moved_window)


def solution(mesh):
    in_specs = (
        P("rep", "tp"),
        P("rep", "tp"),
        P("rep", "tp"),
        P("rep"),
        P("rep", None, "tp"),
        P("rep", None, "tp"),
        P("rep", "tp"),
        P("rep", "tp"),
        P("rep", "tp"),
        P(),
        P(),
        P(None, "tp"),
        P("tp"),
        P("rep", "tp"),
        P("tp"),
        P("tp"),
    )
    out_specs = (P("rep", "tp"), P("rep", "tp"), P("rep", None, None, "tp"))
    return jax.shard_map(
        on_device, mesh=mesh, in_specs=in_specs, out_specs=out_specs, check_vma=False
    )
```

profile of v0, /device:TPU:32, one launch (start us, length us, event | category | flops | bytes accessed | tf_op | source)
XLA Modules:
  0.0 192.9 jit_solution(14140378695549050792)
XLA Ops:
  7.3 1.3 fusion.47
  10.6 1.1 dynamic-slice_bitcast_fusion.1
  11.6 3.4 %collective-permute-start.1 = (bf16[1024,256]{1,0:T(8,128)(2,1)S(1)}, bf16[1024,256]{1,0:T(8,128)(2,1)}, u32[]{:S(2)}, u32[]{:S(2)}) collective-permute-start(bf16[1024,256]{1,0:T(8,128)(2,1)S(1)} %dynamic-slice_bitcast_fusion.1), channel_id=1, source_target_pairs={{256,0},{264,8},{272,16},{280,24},{288,32},{296,40},{304,48},{312,... | collective-permute-start | bytes 1572872 | tf_op jit(solution)/shard_map/ppermute | solution.py:19
  16.3 1.4 fusion.33
  17.7 2.4 %collective-permute-start.2 = (bf16[256]{0:T(256)(128)(2,1)}, bf16[256]{0:T(256)(128)(2,1)}, u32[]{:S(2)}, u32[]{:S(2)}) collective-permute-start(bf16[256]{0:T(256)(128)(2,1)} %get-tuple-element.10), channel_id=1, source_target_pairs={{256,0},{264,8},{272,16},{280,24},{288,32},{296,40},{304,48},{312,... | collective-permute-start | bytes 1544 | tf_op jit(solution)/shard_map/ppermute | solution.py:19
  20.2 1.2 fusion.35
  21.4 3.4 %collective-permute-start = (bf16[256]{0:T(256)(128)(2,1)}, bf16[256]{0:T(256)(128)(2,1)}, u32[]{:S(2)}, u32[]{:S(2)}) collective-permute-start(bf16[256]{0:T(256)(128)(2,1)} %fusion.35), channel_id=1, source_target_pairs={{256,0},{264,8},{272,16},{280,24},{288,32},{296,40},{304,48},{312,... | collective-permute-start | bytes 1544 | tf_op jit(solution)/shard_map/ppermute | solution.py:19
  24.8 1.1 dynamic-slice_bitcast_fusion
  25.9 2.4 %collective-permute-start.3 = (bf16[1024,256]{1,0:T(8,128)(2,1)S(1)}, bf16[1024,256]{1,0:T(8,128)(2,1)}, u32[]{:S(2)}, u32[]{:S(2)}) collective-permute-start(bf16[1024,256]{1,0:T(8,128)(2,1)S(1)} %dynamic-slice_bitcast_fusion), channel_id=1, source_target_pairs={{256,0},{264,8},{272,16},{280,24},{288,32},{296,40},{304,48},{312,... | collective-permute-start | bytes 1572872 | tf_op jit(solution)/shard_map/ppermute | solution.py:19
  28.9 3.4 %collective-permute-start.4 = (bf16[256]{0:T(256)(128)(2,1)}, bf16[256]{0:T(256)(128)(2,1)}, u32[]{:S(2)}, u32[]{:S(2)}) collective-permute-start(bf16[256]{0:T(256)(128)(2,1)} %get-tuple-element.12), channel_id=1, source_target_pairs={{256,0},{264,8},{272,16},{280,24},{288,32},{296,40},{304,48},{312,... | collective-permute-start | bytes 1544 | tf_op jit(solution)/shard_map/ppermute | solution.py:19
  36.0 0.7 constant_dynamic-slice_fusion.10
  37.3 0.7 constant_dynamic-slice_fusion.7
  38.1 1.0 constant_dynamic-slice_fusion.6
  41.2 1.8 copy.50
  43.0 2.0 %fusion.24 = (f32[260]{0:T(512)S(1)}, f32[260]{0:T(512)S(1)}) fusion(s32[4]{0:T(128)S(1)} %iota.55, s32[256]{0:T(256)} %get-tuple-element.30, s32[]{:T(128)} %bitcast.6, s32[256]{0:T(256)} %get-tuple-element.29, s32[]{:T(128)} %bitcast.15), kind=kLoop, calls=%fused_computation.60 | loop fusion | flops 1560 | bytes 4152 | tf_op jit(solution)/shard_map/convert_element_type | solution.py:74
  45.0 1.5 pad_maximum_fusion.2
  46.5 3.0 %subtract_select_fusion = f32[2,512,512]{1,2,0:T(8,128)} fusion(f32[512,512]{0,1:T(8,128)S(1)} %subtract_convert_fusion, f32[2]{0:T(128)} %multiply_exponential_fusion, pred[512,512]{0,1:T(8,128)(4,1)S(1)} %fusion.2, bf16[512,256]{1,0:T(8,128)(2,1)} %param.17, bf16[512,256]{1,0:T(8,128)(2,1)} %param.16), kind=kOutput, calls=%fused_computation.3 | convolution fusion | flops 136314880 | bytes 3932168 | tf_op jit(solution)/shard_map/qhd,khd->hqk/dot_general | solution.py:40
  49.5 2.0 %fusion.48 = f32[2,512]{1,0:T(2,128)S(1)} fusion(f32[512,512]{0,1:T(8,128)S(1)} %subtract_convert_fusion, f32[2]{0:T(128)S(1)} %copy-done.4, pred[512,512]{0,1:T(8,128)(4,1)S(1)} %fusion.2, bf16[512,256]{1,0:T(8,128)(2,1)} %param.17, bf16[512,256]{1,0:T(8,128)(2,1)} %param.16), kind=kOutput, calls=%fused_computation.90 | convolution fusion | flops 137363968 | bytes 1839112 | tf_op jit(solution)/shard_map/sub | solution.py:30
  51.6 3.0 %convolution_convert_fusion = bf16[2,512,128]{1,2,0:T(8,128)(2,1)S(1)} fusion(bf16[512,2,128]{0,2,1:T(8,128)(2,1)} %bitcast.98, f32[2,512]{1,0:T(2,128)S(1)} %fusion.48, f32[2,512,512]{1,2,0:T(8,128)} %subtract_select_fusion), kind=kOutput, calls=%fused_computation.6 | convolution fusion | flops 135923200 | bytes 2625536 | tf_op jit(solution)/shard_map/hqk,khd->qhd/dot_general | solution.py:49
  54.6 0.9 constant_dynamic-slice_fusion.3
  55.7 0.7 slice.18
  56.4 0.8 pad_maximum_fusion.3
  57.2 0.8 fusion.9
  58.9 0.9 constant_dynamic-slice_fusion.1
  60.8 0.8 pad_maximum_fusion.4
  61.9 0.8 pad_maximum_fusion
  64.1 0.9 copy.36
  65.0 75.5 %all-gather.2.cloned.1.call-done = bf16[514,2048]{0,1:T(8,128)(2,1)} async-done(((bf16[514,256]{0,1:T(8,128)(2,1)}), bf16[514,2048]{0,1:T(8,128)(2,1)}) %all-gather.2.cloned.1.call-update) | async-done | bytes 2105360 | tf_op jit(solution)/shard_map/all_gather | solution.py:135
  140.5 2.7 %fusion.53 = (f32[514]{0:T(1024)S(1)}, f32[514,256]{1,0:T(8,128)S(1)}) fusion(bf16[514,256]{1,0:T(8,128)(2,1)S(1)} %copy-done.8, f32[256]{0:T(256)S(1)} %copy-done.9, bf16[514,2048]{0,1:T(8,128)(2,1)} %all-gather.2.cloned.1.call-done, bf16[2048,256]{1,0:T(8,128)(2,1)S(1)} %copy-done), kind=kOutput, calls=%fused_computation.91 | convolution fusion | flops 539493888 | bytes 3946504 | tf_op jit(solution)/shard_map/dot_general | solution.py:134
  143.2 19.9 %psum.14 = f32[514]{0:T(1024)S(1)} all-reduce(f32[514]{0:T(1024)S(1)} %get-tuple-element.27), channel_id=1, replica_groups=mesh['rep'=64,'tp'=8] {'tp'}, use_global_device_ids=true, to_apply=%region_7.8 | all-reduce | flops 514 | bytes 4112 | tf_op jit(solution)/shard_map/psum | solution.py:142
  163.3 21.8 %psum.15 = f32[514]{0:T(1024)S(1)} all-reduce(f32[514]{0:T(1024)S(1)} %multiply_reduce_fusion), channel_id=1, replica_groups=mesh['rep'=64,'tp'=8] {'tp'}, use_global_device_ids=true, to_apply=%region_9.10 | all-reduce | flops 514 | bytes 4112 | tf_op jit(solution)/shard_map/psum | solution.py:144
  185.1 1.0 add_convert_fusion
  (67 shorter events, 7.3 us)
Async XLA Ops:
  7.2 133.3 %copy-start = (bf16[2048,256]{1,0:T(8,128)(2,1)S(1)}, bf16[2048,256]{1,0:T(8,128)(2,1)}, u32[]{:S(2)}) copy-start(bf16[2048,256]{1,0:T(8,128)(2,1)} %param.27) | copy-start | bytes 3145732
  7.2 21.1 %copy-start.3 = (bf16[2,256]{1,0:T(2,128)(2,1)S(1)}, bf16[2,256]{1,0:T(2,128)(2,1)}, u32[]{:S(2)}) copy-start(bf16[2,256]{1,0:T(2,128)(2,1)} %param.24) | copy-start | bytes 3076
  7.2 25.8 %copy-start.5 = (s32[128]{0:T(128)S(1)}, s32[128]{0:T(128)}, u32[]{:S(2)}) copy-start(s32[128]{0:T(128)} %param.25) | copy-start | bytes 1540
  7.2 133.3 %all-gather.2.cloned.1.call-start = ((), (), s32[]{:S(2)}) async-start(), calls=%async_computation | async-start | bytes 2949120 | tf_op jit(solution)/shard_map/all_gather | solution.py:135
  10.5 29.0 %copy-start.2 = (bf16[2,256]{1,0:T(2,128)(2,1)S(1)}, bf16[2,256]{1,0:T(2,128)(2,1)}, u32[]{:S(2)}) copy-start(bf16[2,256]{1,0:T(2,128)(2,1)} %param.22) | copy-start | bytes 3076
  11.6 42.9 %collective-permute-start.1 = (bf16[1024,256]{1,0:T(8,128)(2,1)S(1)}, bf16[1024,256]{1,0:T(8,128)(2,1)}, u32[]{:S(2)}, u32[]{:S(2)}) collective-permute-start(bf16[1024,256]{1,0:T(8,128)(2,1)S(1)} %dynamic-slice_bitcast_fusion.1), channel_id=1, source_target_pairs={{256,0},{264,8},{272,16},{280,24},{288,32},{296,40},{304,48},{312,... | collective-permute-start | bytes 1572872 | tf_op jit(solution)/shard_map/ppermute | solution.py:19
  17.7 38.7 %collective-permute-start.2 = (bf16[256]{0:T(256)(128)(2,1)}, bf16[256]{0:T(256)(128)(2,1)}, u32[]{:S(2)}, u32[]{:S(2)}) collective-permute-start(bf16[256]{0:T(256)(128)(2,1)} %get-tuple-element.10), channel_id=1, source_target_pairs={{256,0},{264,8},{272,16},{280,24},{288,32},{296,40},{304,48},{312,... | collective-permute-start | bytes 1544 | tf_op jit(solution)/shard_map/ppermute | solution.py:19
  21.4 35.8 %collective-permute-start = (bf16[256]{0:T(256)(128)(2,1)}, bf16[256]{0:T(256)(128)(2,1)}, u32[]{:S(2)}, u32[]{:S(2)}) collective-permute-start(bf16[256]{0:T(256)(128)(2,1)} %fusion.35), channel_id=1, source_target_pairs={{256,0},{264,8},{272,16},{280,24},{288,32},{296,40},{304,48},{312,... | collective-permute-start | bytes 1544 | tf_op jit(solution)/shard_map/ppermute | solution.py:19
  25.9 33.0 %collective-permute-start.3 = (bf16[1024,256]{1,0:T(8,128)(2,1)S(1)}, bf16[1024,256]{1,0:T(8,128)(2,1)}, u32[]{:S(2)}, u32[]{:S(2)}) collective-permute-start(bf16[1024,256]{1,0:T(8,128)(2,1)S(1)} %dynamic-slice_bitcast_fusion), channel_id=1, source_target_pairs={{256,0},{264,8},{272,16},{280,24},{288,32},{296,40},{304,48},{312,... | collective-permute-start | bytes 1572872 | tf_op jit(solution)/shard_map/ppermute | solution.py:19
  28.9 31.9 %collective-permute-start.4 = (bf16[256]{0:T(256)(128)(2,1)}, bf16[256]{0:T(256)(128)(2,1)}, u32[]{:S(2)}, u32[]{:S(2)}) collective-permute-start(bf16[256]{0:T(256)(128)(2,1)} %get-tuple-element.12), channel_id=1, source_target_pairs={{256,0},{264,8},{272,16},{280,24},{288,32},{296,40},{304,48},{312,... | collective-permute-start | bytes 1544 | tf_op jit(solution)/shard_map/ppermute | solution.py:19
  46.5 3.0 %copy-start.4 = (f32[2]{0:T(128)S(1)}, f32[2]{0:T(128)}, u32[]{:S(2)}) copy-start(f32[2]{0:T(128)} %multiply_exponential_fusion) | copy-start | bytes 28
  51.6 6.9 %copy-start.1 = (bf16[260,2,128]{2,1,0:T(2,128)(2,1)S(1)}, bf16[260,2,128]{2,1,0:T(2,128)(2,1)}, u32[]{:S(2)}) copy-start(bf16[260,2,128]{2,1,0:T(2,128)(2,1)} %pad_maximum_fusion.2) | copy-start | bytes 399364
  57.2 83.3 %copy-start.8 = (bf16[514,256]{1,0:T(8,128)(2,1)S(1)}, bf16[514,256]{1,0:T(8,128)(2,1)}, u32[]{:S(2)}) copy-start(bf16[514,256]{1,0:T(8,128)(2,1)} %param.29) | copy-start | bytes 789508
  57.2 83.3 %copy-start.9 = (f32[256]{0:T(256)S(1)}, f32[256]{0:T(256)}, u32[]{:S(2)}) copy-start(f32[256]{0:T(256)} %param.28) | copy-start | bytes 3076
  65.0 120.1 %copy-start.6 = (f32[256]{0:T(256)S(1)}, f32[256]{0:T(256)}, u32[]{:S(2)}) copy-start(f32[256]{0:T(256)} %param.31) | copy-start | bytes 3076
  65.0 120.1 %copy-start.7 = (f32[256]{0:T(256)S(1)}, f32[256]{0:T(256)}, u32[]{:S(2)}) copy-start(f32[256]{0:T(256)} %param.30) | copy-start | bytes 3076
Sparse Core Ops, SparseCore 0:
  62.9 77.5 all-gather.1
where the time goes:
time: 194 us; the launch traced here: 193 us
  waiting for transfers between devices  75.5 us (39%)
  blocking collectives  41.6 us (21%)
  between operations  21.3 us (11%)
  local copies, waits for them, and re-layouts  17.8 us (9%)
  starting transfers between devices  15.1 us (8%)
  matrix products  11.9 us (6%)
  other arithmetic  9.62 us (5%)
    all_gather x1, waiting for transfers between devices, on_device(): lax.all_gather(mixed_rows, 'tp', axis=1, tiled=True)  75.5 us
    psum x1, blocking collectives, on_device(): row_var = lax.psum(jnp.sum(centered * centered, axis=1), 'tp') / D  21.8 us
    psum x1, blocking collectives, on_device(): row_mean = lax.psum(row_total, 'tp') / D  19.9 us
    ppermute x5, starting transfers between devices, from_behind(): return lax.ppermute(block, axis, route)  15.1 us
  transfers between devices with their start and end apart: 6, of which 1 were waited for; matrix products, arithmetic and copies ran while one was open for 16% of the time, Pallas kernels for 0%

commit v1 on v0

--- a/solution.py
+++ b/solution.py
@@ -132,7 +132,12 @@
     come_out = decode_attend(come_query, come_keys, come_values, come_len, slopes)
     mixed_rows = jnp.concatenate([prompt_mix, stay_out[None], come_out[None]], axis=0)
     projected = jnp.dot(
-        lax.all_gather(mixed_rows, "tp", axis=1, tiled=True),
+        jnp.concatenate(
+            jax.lax.all_to_all(
+                jnp.stack([mixed_rows] * jax.lax.axis_size("tp"), axis=0), "tp", 0, 0
+            ),
+            axis=1,
+        ),
         out_weight,
         preferred_element_type=jnp.float32,
     )

time: 194 us -> 139 us (0.72)
  the two profiles are of different devices: /device:TPU:32 before, /device:TPU:96 now
where the time goes in v1:
time: 139 us; the launch traced here: 138 us
  blocking collectives  41.7 us (30%)
  waiting for transfers between devices  25.2 us (18%)
  starting transfers between devices  21.8 us (16%)
  local copies, waits for them, and re-layouts  21.6 us (16%)
  other arithmetic  10.1 us (7%)
  matrix products  10.1 us (7%)
  between operations  7.96 us (6%)
    all_to_all x1, waiting for transfers between devices, on_device(): jax.lax.all_to_all(jnp.stack([mixed_rows] * jax.lax.axis_size('tp'), axis...  25.2 us
    psum x1, blocking collectives, on_device(): row_var = lax.psum(jnp.sum(centered * centered, axis=1), 'tp') / D  21.1 us
    psum x1, blocking collectives, on_device(): row_mean = lax.psum(row_total, 'tp') / D  20.5 us
    ppermute x5, starting transfers between devices, from_behind(): return lax.ppermute(block, axis, route)  15.2 us
    all_to_all x1, starting transfers between devices, on_device(): jax.lax.all_to_all(jnp.stack([mixed_rows] * jax.lax.axis_size('tp'), axis...  6.64 us
    dynamic_slice x3, local copies, waits for them, and re-layouts, select_slot(): return lax.dynamic_index_in_dim(stacked, slot_index, 0, keepdims=False)  3.85 us
    concatenate x4, other arithmetic, window_rows(): return jnp.concatenate([cache_rows[:SINK], middle, newest[None]], axis=0)  3.29 us
    dot_general x1, matrix products, prompt_attend(): jnp.einsum('hqk,khd->qhd', weights, value_heads, preferred_element_type=j...  3.01 us
  transfers between devices with their start and end apart: 6, of which 1 were waited for; matrix products, arithmetic and copies ran while one was open for 24% of the time, Pallas kernels for 0%

profile of v1, /device:TPU:96, one launch (start us, length us, event | category | flops | bytes accessed | tf_op | source)
XLA Modules:
  0.0 138.5 jit_solution(8724017512958162649)
XLA Ops:
  0.7 1.3 fusion.47
  5.3 1.3 fusion.33
  6.6 3.4 %collective-permute-start.2 = (bf16[256]{0:T(256)(128)(2,1)}, bf16[256]{0:T(256)(128)(2,1)}, u32[]{:S(2)}, u32[]{:S(2)}) collective-permute-start(bf16[256]{0:T(256)(128)(2,1)} %get-tuple-element.13), channel_id=1, source_target_pairs={{256,0},{264,8},{272,16},{280,24},{288,32},{296,40},{304,48},{312,... | collective-permute-start | bytes 1544 | tf_op jit(solution)/shard_map/ppermute | solution.py:19
  10.0 1.4 fusion.34
  11.3 2.4 %collective-permute-start.4 = (bf16[256]{0:T(256)(128)(2,1)}, bf16[256]{0:T(256)(128)(2,1)}, u32[]{:S(2)}, u32[]{:S(2)}) collective-permute-start(bf16[256]{0:T(256)(128)(2,1)} %get-tuple-element.15), channel_id=1, source_target_pairs={{256,0},{264,8},{272,16},{280,24},{288,32},{296,40},{304,48},{312,... | collective-permute-start | bytes 1544 | tf_op jit(solution)/shard_map/ppermute | solution.py:19
  13.8 1.2 fusion.35
  15.0 3.5 %collective-permute-start = (bf16[256]{0:T(256)(128)(2,1)}, bf16[256]{0:T(256)(128)(2,1)}, u32[]{:S(2)}, u32[]{:S(2)}) collective-permute-start(bf16[256]{0:T(256)(128)(2,1)} %fusion.35), channel_id=1, source_target_pairs={{256,0},{264,8},{272,16},{280,24},{288,32},{296,40},{304,48},{312,... | collective-permute-start | bytes 1544 | tf_op jit(solution)/shard_map/ppermute | solution.py:19
  18.5 1.1 dynamic-slice_bitcast_fusion.1
  19.6 2.4 %collective-permute-start.1 = (bf16[1024,256]{1,0:T(8,128)(2,1)S(1)}, bf16[1024,256]{1,0:T(8,128)(2,1)}, u32[]{:S(2)}, u32[]{:S(2)}) collective-permute-start(bf16[1024,256]{1,0:T(8,128)(2,1)S(1)} %dynamic-slice_bitcast_fusion.1), channel_id=1, source_target_pairs={{256,0},{264,8},{272,16},{280,24},{288,32},{296,40},{304,48},{312,... | collective-permute-start | bytes 1572872 | tf_op jit(solution)/shard_map/ppermute | solution.py:19
  22.0 1.1 dynamic-slice_bitcast_fusion
  23.1 3.4 %collective-permute-start.3 = (bf16[1024,256]{1,0:T(8,128)(2,1)S(1)}, bf16[1024,256]{1,0:T(8,128)(2,1)}, u32[]{:S(2)}, u32[]{:S(2)}) collective-permute-start(bf16[1024,256]{1,0:T(8,128)(2,1)S(1)} %dynamic-slice_bitcast_fusion), channel_id=1, source_target_pairs={{256,0},{264,8},{272,16},{280,24},{288,32},{296,40},{304,48},{312,... | collective-permute-start | bytes 1572872 | tf_op jit(solution)/shard_map/ppermute | solution.py:19
  34.1 1.0 constant_dynamic-slice_fusion.6
  35.8 0.8 fusion.2
  36.6 1.8 %copy.63 = bf16[512,256]{0,1:T(8,128)(2,1)} copy(bf16[512,256]{1,0:T(8,128)(2,1)} %param.18) | data formatting | bytes 524288 | tf_op jit(solution)/shard_map/reshape | solution.py:39
  38.4 2.0 %fusion.24 = (f32[260]{0:T(512)S(1)}, f32[260]{0:T(512)S(1)}) fusion(s32[4]{0:T(128)S(1)} %iota.55, s32[256]{0:T(256)} %get-tuple-element.33, s32[]{:T(128)} %bitcast.6, s32[256]{0:T(256)} %get-tuple-element.32, s32[]{:T(128)} %bitcast.15), kind=kLoop, calls=%fused_computation.60 | loop fusion | flops 1560 | bytes 4152 | tf_op jit(solution)/shard_map/convert_element_type | solution.py:74
  40.4 1.5 %pad_maximum_fusion.2 = bf16[260,2,128]{2,1,0:T(2,128)(2,1)} fusion(bf16[1,2,128]{2,1,0:T(2,128)(2,1)} %bitcast.107, bf16[255,2,128]{2,1,0:T(2,128)(2,1)S(1)} %concatenate.67, bf16[4,2,128]{2,1,0:T(2,128)(2,1)S(1)} %concatenate.66), kind=kLoop, calls=%fused_computation.31 | loop fusion | flops 133120 | bytes 266240 | tf_op jit(solution)/shard_map/concatenate | solution.py:57
  41.9 3.0 %subtract_select_fusion = f32[2,512,512]{1,2,0:T(8,128)} fusion(f32[512,512]{0,1:T(8,128)S(1)} %subtract_convert_fusion, f32[2]{0:T(128)} %multiply_exponential_fusion, pred[512,512]{0,1:T(8,128)(4,1)S(1)} %fusion.2, bf16[512,256]{1,0:T(8,128)(2,1)} %param.17, bf16[512,256]{1,0:T(8,128)(2,1)} %param.16), kind=kOutput, calls=%fused_computation.3 | convolution fusion | flops 136314880 | bytes 3932168 | tf_op jit(solution)/shard_map/qhd,khd->hqk/dot_general | solution.py:40
  44.9 2.0 %fusion.48 = f32[2,512]{1,0:T(2,128)S(1)} fusion(f32[512,512]{0,1:T(8,128)S(1)} %subtract_convert_fusion, f32[2]{0:T(128)S(1)} %copy-done.3, pred[512,512]{0,1:T(8,128)(4,1)S(1)} %fusion.2, bf16[512,256]{1,0:T(8,128)(2,1)} %param.17, bf16[512,256]{1,0:T(8,128)(2,1)} %param.16), kind=kOutput, calls=%fused_computation.90 | convolution fusion | flops 137363968 | bytes 1839112 | tf_op jit(solution)/shard_map/sub | solution.py:30
  47.0 3.0 %convolution_convert_fusion = bf16[2,512,128]{1,2,0:T(8,128)(2,1)S(1)} fusion(bf16[512,2,128]{0,2,1:T(8,128)(2,1)} %bitcast.105, f32[2,512]{1,0:T(2,128)S(1)} %fusion.48, f32[2,512,512]{1,2,0:T(8,128)} %subtract_select_fusion), kind=kOutput, calls=%fused_computation.6 | convolution fusion | flops 135923200 | bytes 2625536 | tf_op jit(solution)/shard_map/hqk,khd->qhd/dot_general | solution.py:49
  50.0 0.9 constant_dynamic-slice_fusion.3
  51.8 0.8 pad_maximum_fusion.3
  52.6 0.8 fusion.9
  54.3 0.9 constant_dynamic-slice_fusion.1
  56.2 0.8 pad_maximum_fusion.4
  57.6 1.5 %stack.8 = bf16[8,514,256]{2,1,0:T(8,128)(2,1)} broadcast(bf16[514,256]{1,0:T(8,128)(2,1)S(1)} %copy.47), dimensions={1,2} | broadcast | bytes 2368512 | tf_op jit(solution)/shard_map/stack | solution.py:137
  59.1 6.6 %all-to-all-start = ((bf16[8,514,256]{2,1,0:T(8,128)(2,1)}), bf16[8,514,256]{2,1,0:T(8,128)(2,1)S(1)}, u32[]{:S(2)}, u32[]{:S(2)}) async-start(bf16[8,514,256]{2,1,0:T(8,128)(2,1)} %stack.8), calls=%async_computation | async-start | bytes 4259840 | tf_op jit(solution)/shard_map/all_to_all | solution.py:136
  67.0 0.9 copy.49
  68.0 25.2 %all-to-all-done = bf16[8,514,256]{2,1,0:T(8,128)(2,1)S(1)} async-done(((bf16[8,514,256]{2,1,0:T(8,128)(2,1)}), bf16[8,514,256]{2,1,0:T(8,128)(2,1)S(1)}, u32[]{:S(2)}, u32[]{:S(2)}) %all-to-all-start) | async-done | bytes 2105376 | tf_op jit(solution)/shard_map/all_to_all | solution.py:136
  94.7 0.9 fusion.53
  95.5 20.5 %psum.14 = f32[514]{0:T(1024)S(1)} all-reduce(f32[514]{0:T(1024)S(1)} %get-tuple-element.30), channel_id=1, replica_groups=mesh['rep'=64,'tp'=8] {'tp'}, use_global_device_ids=true, to_apply=%region_7.8 | all-reduce | flops 514 | bytes 4112 | tf_op jit(solution)/shard_map/psum | solution.py:147
  116.4 21.1 %psum.15 = f32[514]{0:T(1024)S(1)} all-reduce(f32[514]{0:T(1024)S(1)} %multiply_reduce_fusion), channel_id=1, replica_groups=mesh['rep'=64,'tp'=8] {'tp'}, use_global_device_ids=true, to_apply=%region_9.10 | all-reduce | flops 514 | bytes 4112 | tf_op jit(solution)/shard_map/psum | solution.py:149
  137.5 1.0 add_convert_fusion
  (69 shorter events, 10.8 us)
Async XLA Ops:
  0.6 93.8 %copy-start = (bf16[2048,256]{1,0:T(8,128)(2,1)S(1)}, bf16[2048,256]{1,0:T(8,128)(2,1)}, u32[]{:S(2)}) copy-start(bf16[2048,256]{1,0:T(8,128)(2,1)} %param.27) | copy-start | bytes 3145732
  0.6 26.5 %copy-start.4 = (s32[128]{0:T(128)S(1)}, s32[128]{0:T(128)}, u32[]{:S(2)}) copy-start(s32[128]{0:T(128)} %param.25) | copy-start | bytes 1540
  6.6 45.2 %collective-permute-start.2 = (bf16[256]{0:T(256)(128)(2,1)}, bf16[256]{0:T(256)(128)(2,1)}, u32[]{:S(2)}, u32[]{:S(2)}) collective-permute-start(bf16[256]{0:T(256)(128)(2,1)} %get-tuple-element.13), channel_id=1, source_target_pairs={{256,0},{264,8},{272,16},{280,24},{288,32},{296,40},{304,48},{312,... | collective-permute-start | bytes 1544 | tf_op jit(solution)/shard_map/ppermute | solution.py:19
  11.3 44.9 %collective-permute-start.4 = (bf16[256]{0:T(256)(128)(2,1)}, bf16[256]{0:T(256)(128)(2,1)}, u32[]{:S(2)}, u32[]{:S(2)}) collective-permute-start(bf16[256]{0:T(256)(128)(2,1)} %get-tuple-element.15), channel_id=1, source_target_pairs={{256,0},{264,8},{272,16},{280,24},{288,32},{296,40},{304,48},{312,... | collective-permute-start | bytes 1544 | tf_op jit(solution)/shard_map/ppermute | solution.py:19
  15.0 20.7 %copy-start.2 = (bf16[2,256]{1,0:T(2,128)(2,1)S(1)}, bf16[2,256]{1,0:T(2,128)(2,1)}, u32[]{:S(2)}) copy-start(bf16[2,256]{1,0:T(2,128)(2,1)} %param.22) | copy-start | bytes 3076
  15.0 37.6 %collective-permute-start = (bf16[256]{0:T(256)(128)(2,1)}, bf16[256]{0:T(256)(128)(2,1)}, u32[]{:S(2)}, u32[]{:S(2)}) collective-permute-start(bf16[256]{0:T(256)(128)(2,1)} %fusion.35), channel_id=1, source_target_pairs={{256,0},{264,8},{272,16},{280,24},{288,32},{296,40},{304,48},{312,... | collective-permute-start | bytes 1544 | tf_op jit(solution)/shard_map/ppermute | solution.py:19
  19.6 30.4 %collective-permute-start.1 = (bf16[1024,256]{1,0:T(8,128)(2,1)S(1)}, bf16[1024,256]{1,0:T(8,128)(2,1)}, u32[]{:S(2)}, u32[]{:S(2)}) collective-permute-start(bf16[1024,256]{1,0:T(8,128)(2,1)S(1)} %dynamic-slice_bitcast_fusion.1), channel_id=1, source_target_pairs={{256,0},{264,8},{272,16},{280,24},{288,32},{296,40},{304,48},{312,... | collective-permute-start | bytes 1572872 | tf_op jit(solution)/shard_map/ppermute | solution.py:19
  23.1 31.2 %collective-permute-start.3 = (bf16[1024,256]{1,0:T(8,128)(2,1)S(1)}, bf16[1024,256]{1,0:T(8,128)(2,1)}, u32[]{:S(2)}, u32[]{:S(2)}) collective-permute-start(bf16[1024,256]{1,0:T(8,128)(2,1)S(1)} %dynamic-slice_bitcast_fusion), channel_id=1, source_target_pairs={{256,0},{264,8},{272,16},{280,24},{288,32},{296,40},{304,48},{312,... | collective-permute-start | bytes 1572872 | tf_op jit(solution)/shard_map/ppermute | solution.py:19
  41.9 3.0 %copy-start.3 = (f32[2]{0:T(128)S(1)}, f32[2]{0:T(128)}, u32[]{:S(2)}) copy-start(f32[2]{0:T(128)} %multiply_exponential_fusion) | copy-start | bytes 28
  47.0 6.9 %copy-start.1 = (bf16[260,2,128]{2,1,0:T(2,128)(2,1)S(1)}, bf16[260,2,128]{2,1,0:T(2,128)(2,1)}, u32[]{:S(2)}) copy-start(bf16[260,2,128]{2,1,0:T(2,128)(2,1)} %pad_maximum_fusion.2) | copy-start | bytes 399364
  59.1 34.0 %all-to-all-start = ((bf16[8,514,256]{2,1,0:T(8,128)(2,1)}), bf16[8,514,256]{2,1,0:T(8,128)(2,1)S(1)}, u32[]{:S(2)}, u32[]{:S(2)}) async-start(bf16[8,514,256]{2,1,0:T(8,128)(2,1)} %stack.8), calls=%async_computation | async-start | bytes 4259840 | tf_op jit(solution)/shard_map/all_to_all | solution.py:136
  93.7 1.0 copy-start.7
  93.7 0.9 copy-start.8
  94.7 42.8 %copy-start.5 = (f32[256]{0:T(256)S(1)}, f32[256]{0:T(256)}, u32[]{:S(2)}) copy-start(f32[256]{0:T(256)} %param.31) | copy-start | bytes 3076
  94.7 42.8 %copy-start.6 = (f32[256]{0:T(256)S(1)}, f32[256]{0:T(256)}, u32[]{:S(2)}) copy-start(f32[256]{0:T(256)} %param.30) | copy-start | bytes 3076
